TPU v7x, 256 devices: a whole 4x4x8 slice. The times are simulated.
256 devices in a mesh: seq: 32 (over y, x, core), tp: 8 (over z).
Axes of the slice: x: 4, y: 4, z: 8, core: 2. Of those that a mesh axis runs over, the one named last changes fastest.
Arguments:
- queries: bfloat16 [32, 64, 4096], P('seq', None, 'tp'), may hold values from -8 to 8
- draft_kv: bfloat16 [32, 64, 8, 128], P('seq', None, 'tp'), may hold values from -12.5 to 12.5
- cache_kv: bfloat16 [8, 16384, 8, 128], P(None, 'seq', 'tp'), may hold values from -10 to 10
- cache_len: int32 [8], replicated, may hold values from 4096 to 16384
- group_of: int32 [32], replicated, may hold values from 0 to 7, as said below
- parents: int32 [32, 64], P('seq'), may hold values from 0 to 62, as said below
- sink_logit: float32 [64], P('tp'), may hold values from 4 to 20
- w_out: bfloat16 [4096, 2880], P('tp'), may hold values from -0.09375 to 0.09375
- hidden_in: bfloat16 [2048, 2880], P('seq', 'tp'), may hold values from -3 to 3
- norm_gain: float32 [2880], replicated, may hold values from 0.5 to 1.5
- routes: int32 [2048, 4], P('seq'), may hold values from 0 to 31, all different within a row; in each aligned block of 64 rows (0 to 63, 64 to 127, ...) at most 16 rows name the same one
- route_weight: float32 [2048, 4], P('seq'), may hold values from 0.1 to 1
- w_gate_up: bfloat16 [32, 2, 2880, 2880], P('seq', None, None, 'tp'), may hold values from -0.109375 to 0.109375
- w_down: bfloat16 [32, 2880, 2880], P('seq', 'tp'), may hold values from -0.109375 to 0.109375
- accepted_idx: int32 [32, 16], P('seq'), may hold values from 0 to 45, as said below
- accepted_len: int32 [32], P('seq'), may hold values from 1 to 16, as said below
- tail_slot: int32 [32], replicated, may hold values from 0 to 31, each once
Outputs:
- out_hidden: bfloat16 [2048, 2880], P('seq', 'tp')
- new_tail: bfloat16 [32, 16, 8, 128], P('seq', None, 'tp')
Inputs may be any that keep to these rules, and one draw needn't show every extreme that they name: `parents`: node 0 of every tree is its root and its own parent; every other node's parent is one of the three nodes before it. `accepted_idx`: row r lists the first 16 nodes of a path from the root of request r's tree down to one of its last four nodes, root first. `accepted_len`: each request accepts one or more nodes. `group_of`: every prompt group has exactly 4 requests. `routes`: the 4 experts of a token differ; at most 16 of one device's rows (one aligned block of 64 tokens) name one expert.
All inputs are finite; a program needn't handle non-finite values.
Results may differ from a plain program's by a relative error of at most 0.025.
Values may be sent and summed in bfloat16 or wider, within the bound.
A program may use at most 128 MiB of HBM per device.

v0:
```python
import jax
import jax.numpy as jnp
from jax import lax
from jax.sharding import PartitionSpec as P

HQ = 64
KVH = 8
HD = 64


def ancestry(parents):
    tree_len = parents.shape[1]
    node_ids = jnp.arange(tree_len, dtype=jnp.int32)
    linked = (parents[:, :, None] == node_ids[None, None, :]) | (
        node_ids[:, None] == node_ids[None, :]
    )[None]
    reachable = linked.astype(jnp.float32)
    for repeat in range((tree_len - 1).bit_length()):
        reachable = jnp.minimum(
            jnp.einsum("rij,rjk->rik", reachable, reachable, precision=lax.Precision.HIGHEST), 1.0
        )
    return reachable


def cache_block(block_queries, block_groups, cache_kv, cache_len, positions):
    block_rows, tree_len, head_cols = block_queries.shape
    kv_dev = cache_kv.shape[2]
    grouped = block_queries.reshape(block_rows, tree_len, kv_dev, HQ // KVH, HD)
    picked = jnp.take(cache_kv, block_groups, axis=0)
    cache_keys = picked[..., :HD]
    cache_values = picked[..., HD:]
    scores = (
        jnp.einsum("rtkqd,rckd->rkqtc", grouped, cache_keys, preferred_element_type=jnp.float32)
        * 0.125
    )
    lengths = jnp.take(cache_len, block_groups)
    usable = (positions[None, :] < lengths[:, None])[:, None, None, None, :]
    masked = jnp.where(usable, scores, -1e30)
    shard_max = jnp.max(masked, axis=-1)
    weights = jnp.where(usable, jnp.exp(masked - shard_max[..., None]), 0.0)
    shard_sum = jnp.sum(weights, axis=-1)
    shard_out = jnp.einsum(
        "rkqtc,rckd->rkqtd",
        weights.astype(jnp.bfloat16),
        cache_values,
        preferred_element_type=jnp.float32,
    )
    shard_out = (shard_out / jnp.maximum(shard_sum, 1.0)[..., None]).astype(jnp.bfloat16)
    out_rows = shard_out.transpose(0, 3, 1, 2, 4).reshape(block_rows, tree_len, head_cols)
    max_rows = shard_max.transpose(0, 3, 1, 2).reshape(block_rows, tree_len, -1)
    sum_rows = shard_sum.transpose(0, 3, 1, 2).reshape(block_rows, tree_len, -1)
    return (out_rows, max_rows, sum_rows)


def expert_rows(arrived, w_gate_up, w_down):
    exp_dev = w_gate_up.shape[0]
    sources = arrived.shape[0] // exp_dev
    grouped = arrived.reshape(sources, exp_dev, arrived.shape[1], arrived.shape[2])
    gate_proj = jnp.einsum(
        "sexd,edf->sexf", grouped, w_gate_up[:, 0], preferred_element_type=jnp.float32
    )
    upward = jnp.einsum(
        "sexd,edf->sexf", grouped, w_gate_up[:, 1], preferred_element_type=jnp.float32
    )
    active = (gate_proj * jax.nn.sigmoid(1.702 * gate_proj) * (upward + 1.0)).astype(jnp.bfloat16)
    down_part = jnp.einsum("sexf,efd->sexd", active, w_down, preferred_element_type=jnp.float32)
    return down_part.reshape(arrived.shape[0], arrived.shape[1], -1)


def shards(
    queries,
    draft_kv,
    cache_kv,
    cache_len,
    group_of,
    parents,
    sink_logit,
    w_out,
    hidden_in,
    norm_gain,
    routes,
    route_weight,
    w_gate_up,
    w_down,
    accepted_idx,
    accepted_len,
    tail_slot,
):
    seq_count = lax.axis_size("seq")
    req_dev, tree_len, head_cols = queries.shape
    kv_dev = cache_kv.shape[2]
    per_kv = HQ // KVH
    heads_dev = kv_dev * per_kv
    shard_len = cache_kv.shape[1]
    positions = lax.axis_index("seq") * shard_len + jnp.arange(shard_len, dtype=jnp.int32)
    every_query = lax.all_gather(queries, "seq", axis=0, tiled=True)
    requests_all = every_query.shape[0]
    block_count = requests_all // 8
    stacked = (
        every_query.reshape(block_count, 8, tree_len, head_cols),
        group_of.reshape(block_count, 8),
    )
    shard_out, shard_max, shard_sum = lax.map(
        lambda blocks: cache_block(blocks[0], blocks[1], cache_kv, cache_len, positions), stacked
    )
    shard_out = shard_out.reshape(seq_count, req_dev, tree_len, head_cols)
    shard_max = shard_max.reshape(seq_count, req_dev, tree_len, heads_dev)
    shard_sum = shard_sum.reshape(seq_count, req_dev, tree_len, heads_dev)
    came_out = lax.all_to_all(shard_out, "seq", split_axis=0, concat_axis=0, tiled=True)
    came_max, came_sum = (
        lax.all_to_all(shard_max, "seq", split_axis=0, concat_axis=0, tiled=True),
        lax.all_to_all(shard_sum, "seq", split_axis=0, concat_axis=0, tiled=True),
    )
    reachable = ancestry(parents)
    own_heads = queries.reshape(req_dev, tree_len, kv_dev, per_kv, HD)
    draft_keys = draft_kv[..., :HD]
    draft_values = draft_kv[..., HD:]
    tree_scores = (
        jnp.einsum("rtkqd,rukd->rkqtu", own_heads, draft_keys, preferred_element_type=jnp.float32)
        * 0.125
    )
    allowed = (reachable > 0.5)[:, None, None, :, :]
    tree_masked = jnp.where(allowed, tree_scores, -1e30)
    tree_max = jnp.max(tree_masked, axis=-1)
    tree_weight = jnp.where(allowed, jnp.exp(tree_masked - tree_max[..., None]), 0.0)
    tree_sum = jnp.sum(tree_weight, axis=-1)
    tree_num = jnp.einsum(
        "rkqtu,rukd->rkqtd",
        tree_weight.astype(jnp.bfloat16),
        draft_values,
        preferred_element_type=jnp.float32,
    )
    tree_max = tree_max.transpose(0, 3, 1, 2).reshape(req_dev, tree_len, heads_dev)
    tree_sum = tree_sum.transpose(0, 3, 1, 2).reshape(req_dev, tree_len, heads_dev)
    tree_num = tree_num.transpose(0, 3, 1, 2, 4).reshape(req_dev, tree_len, heads_dev, HD)
    sink_rows = sink_logit[None, None, :]
    ceiling = jnp.maximum(jnp.maximum(jnp.max(came_max, axis=0), tree_max), sink_rows)
    shard_scale = came_sum * jnp.exp(came_max - ceiling[None])
    tree_scale = jnp.exp(tree_max - ceiling)
    denominator = (
        jnp.sum(shard_scale, axis=0) + tree_scale * tree_sum + jnp.exp(sink_rows - ceiling)
    )
    weighted = jnp.sum(
        shard_scale[..., None]
        * came_out.reshape(seq_count, req_dev, tree_len, heads_dev, HD).astype(jnp.float32),
        axis=0,
    )
    numerator = weighted + tree_scale[..., None] * tree_num
    attention = (
        (numerator / denominator[..., None])
        .reshape(req_dev * tree_len, heads_dev * HD)
        .astype(jnp.bfloat16)
    )
    projected = jnp.dot(attention, w_out, preferred_element_type=jnp.float32)
    width_dev = hidden_in.shape[1]
    tp_index = lax.axis_index("tp")
    summed = lax.psum(projected, "tp")
    resid_full = lax.all_gather(hidden_in, "tp", axis=1, tiled=True)
    stream = (resid_full.astype(jnp.float32) + summed).astype(jnp.bfloat16)
    stream_f = stream.astype(jnp.float32)
    inv_scale = lax.rsqrt(jnp.mean(stream_f * stream_f, axis=-1, keepdims=True) + 1e-05)
    normed_full = (stream_f * inv_scale * norm_gain[None, :]).astype(jnp.bfloat16)
    stream_cols = lax.dynamic_slice_in_dim(stream, tp_index * width_dev, width_dev, 1)
    tok_dev = routes.shape[0]
    top_count = routes.shape[1]
    exp_dev = w_gate_up.shape[0]
    experts_all = seq_count * exp_dev
    capacity = 2 * tok_dev * top_count // experts_all
    flat_routes = routes.reshape(-1)
    onehot = (flat_routes[:, None] == jnp.arange(experts_all, dtype=jnp.int32)[None, :]).astype(
        jnp.int32
    )
    position = jnp.sum((jnp.cumsum(onehot, axis=0) - onehot) * onehot, axis=1)
    slot_ids = flat_routes * capacity + position
    buckets = jnp.arange(experts_all * capacity, dtype=jnp.int32)
    placing = jnp.sum(
        (slot_ids.reshape(tok_dev, top_count)[None, :, :] == buckets[:, None, None]).astype(
            jnp.int32
        ),
        axis=2,
    ).astype(jnp.bfloat16)
    dispatched = (
        jnp.dot(placing, normed_full, preferred_element_type=jnp.float32)
        .astype(jnp.bfloat16)
        .reshape(experts_all, capacity, -1)
    )
    down_part = expert_rows(
        lax.all_to_all(dispatched, "seq", split_axis=0, concat_axis=0, tiled=True),
        w_gate_up,
        w_down,
    )
    expert_out = lax.psum_scatter(
        down_part.astype(jnp.bfloat16), "tp", scatter_dimension=2, tiled=True
    )
    returned = lax.all_to_all(expert_out, "seq", split_axis=0, concat_axis=0, tiled=True)
    gathered_rows = jnp.take(
        returned.reshape(experts_all * capacity, -1), slot_ids, axis=0
    ).reshape(tok_dev, top_count, -1)
    mixture = jnp.sum(route_weight[:, :, None] * gathered_rows.astype(jnp.float32), axis=1)
    out_hidden = (stream_cols.astype(jnp.float32) + mixture).astype(jnp.bfloat16)
    blk_len = accepted_idx.shape[1]
    chosen = draft_kv[jnp.arange(req_dev, dtype=jnp.int32)[:, None], accepted_idx]
    kept_rows = jnp.arange(blk_len, dtype=jnp.int32)[None, :] < accepted_len[:, None]
    picked_rows = jnp.where(kept_rows[:, :, None, None], chosen, jnp.zeros_like(chosen))
    everyone = lax.all_gather(picked_rows, "seq", axis=0, tiled=True)
    my_slots = lax.axis_index("seq") * req_dev + jnp.arange(req_dev, dtype=jnp.int32)
    selector = (tail_slot[None, :] == my_slots[:, None]).astype(jnp.bfloat16)
    new_tail = jnp.dot(
        selector, everyone.reshape(everyone.shape[0], -1), preferred_element_type=jnp.float32
    ).astype(jnp.bfloat16)
    new_tail = new_tail.reshape(req_dev, blk_len, kv_dev, -1)
    return (out_hidden, new_tail)


def solution(mesh):
    in_specs = (
        P("seq", None, "tp"),
        P("seq", None, "tp", None),
        P(None, "seq", "tp", None),
        P(),
        P(),
        P("seq", None),
        P("tp"),
        P("tp", None),
        P("seq", "tp"),
        P(),
        P("seq", None),
        P("seq", None),
        P("seq", None, None, "tp"),
        P("seq", "tp", None),
        P("seq", None),
        P("seq"),
        P(),
    )
    out_specs = (P("seq", "tp"), P("seq", None, "tp", None))
    return jax.shard_map(shards, mesh=mesh, in_specs=in_specs, out_specs=out_specs, check_vma=False)
```

profile of v0, /device:TPU:1, one launch (start us, length us, event | category | flops | bytes accessed | tf_op | source)
XLA Modules:
  0.0 533.3 jit_solution(3878875501359007208)
XLA Ops:
  10.3 53.3 %all-gather.3.cloned.1.call-done = bf16[32,64,512]{2,1,0:T(8,128)(2,1)} async-done(((bf16[1,64,512]{2,1,0:T(8,128)(2,1)}), bf16[32,64,512]{2,1,0:T(8,128)(2,1)}) %all-gather.3.cloned.1.call-update) | async-done | bytes 2097168 | tf_op jit(solution)/shard_map/all_gather | solution.py:96
  63.7 97.3 %while.15 = (s32[]{:T(128)}, bf16[4,8,64,512]{3,2,1,0:T(8,128)(2,1)}, f32[4,8,64,8]{2,3,1,0:T(8,128)}, f32[4,8,64,8]{2,3,1,0:T(8,128)}, s32[4,8]{1,0:T(4,128)S(1...) while((s32[]{:T(128)}, ...), condition=%wide.region_3.4_spmd.clone, body=%wide.region_0.3_spmd.clone.sunk | while | flops 565184128 | bytes 43791872 | solution.py:103
  162.7 5.1 all-to-all-start.1
  170.4 4.7 all-to-all-done.1
  175.1 3.9 all-to-all-start
  180.8 5.6 %all-to-all-done = f32[32,1,512]{2,1,0:T(1,128)S(1)} async-done(((f32[32,1,512]{2,1,0:T(1,128)}), f32[32,1,512]{2,1,0:T(1,128)S(1)}, u32[]{:S(2)}, u32[]{:S(2)}) %all-to-all-start) | async-done | bytes 65568 | tf_op jit(solution)/shard_map/all_to_all | solution.py:112
  186.4 4.7 all-to-all-start.2
  193.3 23.3 %all-gather = bf16[8,360,64]{1,2,0:T(8,128)(2,1)S(1)} all-gather(bf16[1,360,64]{1,2,0:T(8,128)(2,1)} %bitcast.318), channel_id=1, replica_groups=mesh['seq'=32,'tp'=8] {'tp'}, dimensions={0}, use_global_device_ids=true | all-gather | bytes 414720 | tf_op jit(solution)/shard_map/all_gather | solution.py:158
  227.4 5.9 %mul.135 = f32[32,64,8,64]{3,2,1,0:T(8,128)} broadcast(f32[32,64,8]{2,1,0:T(8,128)} %copy.92), dimensions={0,1,2} | broadcast | bytes 4259840 | tf_op jit(solution)/shard_map/mul | solution.py:144
  233.4 7.5 %mul.136 = f32[32,1,64,512]{3,2,1,0:T(8,128)} reshape(f32[32,64,8,64]{3,2,1,0:T(8,128)} %mul.135) | data formatting | bytes 8388608 | tf_op jit(solution)/shard_map/mul | solution.py:144
  240.9 3.6 multiply_reduce_fusion
  247.8 72.6 %all-reduce.3.cloned.1.call-done = f32[64,2880]{1,0:T(8,128)} async-done(((f32[64,2880]{1,0:T(8,128)}), f32[64,2880]{1,0:T(8,128)}) %all-reduce.3.cloned.1.call-update) | async-done | bytes 737296 | tf_op jit(solution)/shard_map/psum | solution.py:157
  325.4 4.6 copy.103
  329.9 50.3 %all_to_all.25 = bf16[32,16,2880]{2,1,0:T(8,128)(2,1)S(1)} all-to-all(bf16[32,16,2880]{2,1,0:T(8,128)(2,1)} %bitcast.309), channel_id=1, replica_groups=mesh['seq'=32,'tp'=8] {'seq'}, dimensions={0} | all-to-all | bytes 5898240 | tf_op jit(solution)/shard_map/all_to_all | solution.py:188
  381.9 4.2 fusion.27
  386.1 8.5 %convolution_convert_fusion = bf16[32,16,2880]{2,1,0:T(8,128)(2,1)} fusion(bf16[1,360,2880]{2,1,0:T(8,128)(2,1)} %param.32, bf16[32,16,2880]{2,1,0:T(8,128)(2,1)} %copy-done.2, bf16[1,2,2880,360]{2,3,1,0:T(8,128)(2,1)} %param.31, f32[32,1,16,360]{3,2,0,1:T(8,128)} %fusion.27), kind=kOutput, calls=%fused_computation.40 | convolution fusion | flops 2126315520 | bytes 10989568 | tf_op jit(solution)/shard_map/sexf,efd->sexd/dot_general | solution.py:66
  394.6 21.4 %copy.108 = bf16[32,16,2880]{1,0,2:T(8,128)(2,1)} copy(bf16[32,16,2880]{2,1,0:T(8,128)(2,1)} %convolution_convert_fusion) | data formatting | bytes 5898240
  416.0 39.5 %reshape.749 = bf16[2880,512]{1,0:T(8,128)(2,1)} reshape(bf16[2880,32,16]{2,1,0:T(8,128)(2,1)} %bitcast.306) | data formatting | bytes 5898240
  457.1 22.6 %all_gather.11 = bf16[32,16,1,128]{3,1,2,0:T(8,128)(2,1)S(1)} all-gather(bf16[1,16,1,128]{3,1,2,0:T(8,128)(2,1)S(1)} %bitcast_select_fusion.2), channel_id=1, replica_groups=mesh['seq'=32,'tp'=8] {'seq'}, dimensions={0}, use_global_device_ids=true | all-gather | bytes 135168 | tf_op jit(solution)/shard_map/all_gather | solution.py:205
  479.9 12.3 %reduce-scatter.4.cloned.1.call-done = bf16[360,512]{1,0:T(8,128)(2,1)} async-done(((bf16[2880,512]{1,0:T(8,128)(2,1)}), bf16[360,512]{1,0:T(8,128)(2,1)}) %reduce-scatter.4.cloned.1.call-update) | async-done | bytes 368656
  492.2 4.4 reshape.750
  496.5 5.0 copy.109
  501.6 11.1 %all-to-all-start.4 = ((bf16[32,16,360]{2,1,0:T(8,128)(2,1)}), bf16[32,16,360]{2,1,0:T(8,128)(2,1)S(1)}, u32[]{:S(2)}, u32[]{:S(2)}) async-start(bf16[32,16,360]{2,1,0:T(8,128)(2,1)} %copy.109), calls=%async_computation.4 | async-start | bytes 786432 | tf_op jit(solution)/shard_map/all_to_all | solution.py:195
  514.1 8.7 %all-to-all-done.4 = bf16[32,16,360]{2,1,0:T(8,128)(2,1)S(1)} async-done(((bf16[32,16,360]{2,1,0:T(8,128)(2,1)}), bf16[32,16,360]{2,1,0:T(8,128)(2,1)S(1)}, u32[]{:S(2)}, u32[]{:S(2)}) %all-to-all-start.4) | async-done | bytes 368672 | tf_op jit(solution)/shard_map/all_to_all | solution.py:195
  (202 shorter events, 135.3 us)
Async XLA Ops:
  7.2 237.3 %copy-start = (bf16[512,2880]{0,1:T(8,128)(2,1)S(1)}, bf16[512,2880]{0,1:T(8,128)(2,1)}, u32[]{:S(2)}) copy-start(bf16[512,2880]{0,1:T(8,128)(2,1)} %param.26) | copy-start | bytes 8847364
  7.2 56.5 %all-gather.3.cloned.1.call-start = ((), (), s32[]{:S(2)}) async-start(), calls=%async_computation.6 | async-start | bytes 2162688 | tf_op jit(solution)/shard_map/all_gather | solution.py:96
  63.7 115.5 %copy-start.6 = (bf16[1,64,512]{2,1,0:T(8,128)(2,1)S(1)}, bf16[1,64,512]{2,1,0:T(8,128)(2,1)}, u32[]{:S(2)}) copy-start(bf16[1,64,512]{2,1,0:T(8,128)(2,1)} %param.19) | copy-start | bytes 196612
  63.7 115.6 %copy-start.13 = (s32[64,4]{0,1:T(4,128)S(1)}, s32[64,4]{0,1:T(4,128)}, u32[]{:S(2)}) copy-start(s32[64,4]{0,1:T(4,128)} %param.29) | copy-start | bytes 3076
  78.0 3.0 copy-start.1
  102.3 3.0 copy-start.1
  126.6 3.0 copy-start.1
  150.9 3.0 copy-start.1
  161.0 30.9 %copy-start.7 = (bf16[1,64,1,128]{3,1,2,0:T(8,128)(2,1)S(1)}, bf16[1,64,1,128]{3,1,2,0:T(8,128)(2,1)}, u32[]{:S(2)}) copy-start(bf16[1,64,1,128]{3,1,2,0:T(8,128)(2,1)} %param.20) | copy-start | bytes 49156
  162.7 12.4 %all-to-all-start.1 = ((f32[32,1,512]{2,1,0:T(1,128)}), f32[32,1,512]{2,1,0:T(1,128)S(1)}, u32[]{:S(2)}, u32[]{:S(2)}) async-start(f32[32,1,512]{2,1,0:T(1,128)} %reshape.754), calls=%async_computation.1 | async-start | bytes 131072 | tf_op jit(solution)/shard_map/all_to_all | solution.py:111
  175.1 17.0 %copy-start.9 = (f32[32,1,512]{2,1,0:T(1,128)}, f32[32,1,512]{2,1,0:T(1,128)S(1)}, u32[]{:S(2)}) copy-start(f32[32,1,512]{2,1,0:T(1,128)S(1)} %all-to-all-done.1) | copy-start | bytes 196612
  175.1 11.3 %all-to-all-start = ((f32[32,1,512]{2,1,0:T(1,128)}), f32[32,1,512]{2,1,0:T(1,128)S(1)}, u32[]{:S(2)}, u32[]{:S(2)}) async-start(f32[32,1,512]{2,1,0:T(1,128)} %reshape.752), calls=%async_computation | async-start | bytes 131072 | tf_op jit(solution)/shard_map/all_to_all | solution.py:112
  186.4 4.8 copy-start.11
  186.4 54.4 %all-to-all-start.2 = ((bf16[32,1,64,512]{3,2,1,0:T(8,128)(2,1)}), bf16[32,1,64,512]{3,2,1,0:T(8,128)(2,1)}, u32[]{:S(2)}, u32[]{:S(2)}) async-start(bf16[32,1,64,512]{3,2,1,0:T(8,128)(2,1)} %bitcast.313), calls=%async_computation.2 | async-start | bytes 4194304 | tf_op jit(solution)/shard_map/all_to_all | solution.py:109
  191.2 129.2 %all-reduce.3.cloned.1.call-start = ((), (), s32[]{:S(2)}) async-start(), calls=%async_computation.7 | async-start | bytes 1507328 | tf_op jit(solution)/shard_map/psum | solution.py:157
  192.4 28.8 %copy-start.10 = (f32[32,1,512]{2,1,0:T(1,128)S(1)}, f32[32,1,512]{2,1,0:T(1,128)}, u32[]{:S(2)}) copy-start(f32[32,1,512]{2,1,0:T(1,128)} %copy-done.9) | copy-start | bytes 196612
  193.3 28.8 %copy-start.12 = (f32[32,1,512]{2,1,0:T(1,128)S(1)}, f32[32,1,512]{2,1,0:T(1,128)}, u32[]{:S(2)}) copy-start(f32[32,1,512]{2,1,0:T(1,128)} %copy-done.11) | copy-start | bytes 196612
  240.9 3.6 copy-start.4
  240.9 3.6 copy-start.5
  244.5 78.2 %copy-start.14 = (f32[2880]{0:T(1024)S(1)}, f32[2880]{0:T(1024)}, u32[]{:S(2)}) copy-start(f32[2880]{0:T(1024)} %param.28) | copy-start | bytes 34564
  246.4 245.7 %reduce-scatter.4.cloned.1.call-start = ((), (), s32[]{:S(2)}) async-start(), calls=%async_computation.8 | async-start | bytes 3317760
  455.4 24.3 %copy-start.18 = (s32[32]{0:T(128)S(1)}, s32[32]{0:T(128)}, u32[]{:S(2)}) copy-start(s32[32]{0:T(128)} %param.35) | copy-start | bytes 388
  479.8 33.0 %copy-start.17 = (f32[64,4]{0,1:T(4,128)S(1)}, f32[64,4]{0,1:T(4,128)}, u32[]{:S(2)}) copy-start(f32[64,4]{0,1:T(4,128)} %param.30) | copy-start | bytes 3076
  501.6 21.3 %all-to-all-start.4 = ((bf16[32,16,360]{2,1,0:T(8,128)(2,1)}), bf16[32,16,360]{2,1,0:T(8,128)(2,1)S(1)}, u32[]{:S(2)}, u32[]{:S(2)}) async-start(bf16[32,16,360]{2,1,0:T(8,128)(2,1)} %copy.109), calls=%async_computation.4 | async-start | bytes 786432 | tf_op jit(solution)/shard_map/all_to_all | solution.py:195
  (6 other events, 9.1 us)
Sparse Core Ops, SparseCore 0:
  10.6 53.0 all-gather.2
  246.5 73.8 all-reduce.2
  455.6 36.5 reduce-scatter.3
where the time goes:
time: 536 us; the launch traced here: 533 us
  local copies, waits for them, and re-layouts  164 us (31%)
  waiting for transfers between devices  158 us (29%)
  blocking collectives  96.2 us (18%)
  matrix products  42.4 us (8%)
  other arithmetic  32.4 us (6%)
  starting transfers between devices  25 us (5%)
  between operations  14.9 us (3%)
    unnamed x48, local copies, waits for them, and re-layouts  77 us
    psum x1, waiting for transfers between devices, shards(): summed = lax.psum(projected, 'tp')  72.6 us
    all_gather x1, waiting for transfers between devices, shards(): every_query = lax.all_gather(queries, 'seq', axis=0, tiled=True)  53.3 us
    all_to_all x1, blocking collectives, shards(): lax.all_to_all(dispatched, 'seq', split_axis=0, concat_axis=0, tiled=True)  50.3 us
    all_gather x1, blocking collectives, shards(): resid_full = lax.all_gather(hidden_in, 'tp', axis=1, tiled=True)  23.3 us
    all_gather x1, blocking collectives, shards(): everyone = lax.all_gather(picked_rows, 'seq', axis=0, tiled=True)  22.6 us
    gather x8, local copies, waits for them, and re-layouts, cache_block(): picked = jnp.take(cache_kv, block_groups, axis=0)  20.7 us
    mul x3, local copies, waits for them, and re-layouts, shards(): shard_scale[..., None]  14.9 us
  transfers between devices with their start and end apart: 7, of which 6 were waited for; matrix products, arithmetic and copies ran while one was open for 7% of the time, Pallas kernels for 0%

commit v1 on v0

--- a/solution.py
+++ b/solution.py
@@ -6,6 +6,28 @@
 HQ = 64
 KVH = 8
 HD = 64
+
+
+def laid_out(blocks, dim):
+    shape = list(blocks.shape[1:])
+    shape[dim] *= blocks.shape[0]
+    return jnp.moveaxis(blocks, 0, dim).reshape(shape)
+
+
+def ring_gather(x, axis, dim):
+    size = lax.axis_size(axis)
+    pairs = [(i, (i + 1) % size) for i in range(size)]
+    back = [(b, a) for a, b in pairs]
+    lower, upper = ([], [])
+    for step in range(size - 1):
+        if step % 2 == 0:
+            lower.append(lax.ppermute(lower[-1] if lower else x, axis, pairs))
+        else:
+            upper.append(lax.ppermute(upper[-1] if upper else x, axis, back))
+    blocks = jnp.stack([*lower[::-1], x, *upper])
+    shift = lax.axis_index(axis) - len(lower)
+    blocks = blocks[(jnp.arange(size) - shift) % size]
+    return laid_out(blocks, dim)
 
 
 def ancestry(parents):
@@ -155,7 +177,7 @@
     width_dev = hidden_in.shape[1]
     tp_index = lax.axis_index("tp")
     summed = lax.psum(projected, "tp")
-    resid_full = lax.all_gather(hidden_in, "tp", axis=1, tiled=True)
+    resid_full = ring_gather(hidden_in, "tp", 1)
     stream = (resid_full.astype(jnp.float32) + summed).astype(jnp.bfloat16)
     stream_f = stream.astype(jnp.float32)
     inv_scale = lax.rsqrt(jnp.mean(stream_f * stream_f, axis=-1, keepdims=True) + 1e-05)

time: 536 us -> 515 us (0.961)
  waiting for transfers between devices: 158 us -> 130 us
  blocking collectives: 96.2 us -> 72.9 us
  starting transfers between devices: 25 us -> 39.2 us
  local copies, waits for them, and re-layouts: 164 us -> 178 us
    all_gather x1 -> x0, blocking collectives: 23.3 us -> none  [shards(): resid_full = lax.all_gather(hidden_in, 'tp', axis=1, tiled=True)]
    ppermute x0 -> x7, starting transfers between devices: none -> 14 us  [the longest x3 10.2 us: ring_gather(): upper.append(lax.ppermute(upper[-1] if upper else x, axis, back))]
    all_gather x1, waiting for transfers between devices: 53.3 us -> 39.4 us  [shards(): every_query = lax.all_gather(queries, 'seq', axis=0, tiled=True)]
    psum x1, waiting for transfers between devices: 72.6 us -> 60.7 us  [shards(): summed = lax.psum(projected, 'tp')]
    unnamed x48 -> x47, local copies, waits for them, and re-layouts: 77 us -> 87.6 us
  transfers between devices with their start and end apart: 7 -> 14, of which waited for: 6 -> 6; matrix products, arithmetic and copies ran while one was open for 7% -> 31% of each run, Pallas kernels for 0% -> 0%
where the time goes in v1:
time: 515 us; the launch traced here: 512 us
  local copies, waits for them, and re-layouts  178 us (35%)
  waiting for transfers between devices  130 us (25%)
  blocking collectives  72.9 us (14%)
  matrix products  43.1 us (8%)
  starting transfers between devices  39.2 us (8%)
  other arithmetic  34.5 us (7%)
  between operations  14.9 us (3%)
    unnamed x47, local copies, waits for them, and re-layouts  87.6 us
    psum x1, waiting for transfers between devices, shards(): summed = lax.psum(projected, 'tp')  60.7 us
    all_to_all x1, blocking collectives, shards(): lax.all_to_all(dispatched, 'seq', split_axis=0, concat_axis=0, tiled=True)  50.3 us
    all_gather x1, waiting for transfers between devices, shards(): every_query = lax.all_gather(queries, 'seq', axis=0, tiled=True)  39.4 us
    all_gather x1, blocking collectives, shards(): everyone = lax.all_gather(picked_rows, 'seq', axis=0, tiled=True)  22.6 us
    gather x8, local copies, waits for them, and re-layouts, cache_block(): picked = jnp.take(cache_kv, block_groups, axis=0)  20.7 us
    mul x3, local copies, waits for them, and re-layouts, shards(): shard_scale[..., None]  14.9 us
    unnamed x4, waiting for transfers between devices  13 us
  transfers between devices with their start and end apart: 14, of which 6 were waited for; matrix products, arithmetic and copies ran while one was open for 31% of the time, Pallas kernels for 0%

profile of v1, /device:TPU:1, one launch (start us, length us, event | category | flops | bytes accessed | tf_op | source)
XLA Modules:
  0.0 512.0 jit_solution(12104373467268347964)
XLA Ops:
  10.5 4.0 collective-permute-start.4
  24.3 39.4 %all-gather.2.cloned.1.call-done = bf16[32,64,512]{2,1,0:T(8,128)(2,1)} async-done(((bf16[1,64,512]{2,1,0:T(8,128)(2,1)}), bf16[32,64,512]{2,1,0:T(8,128)(2,1)}) %all-gather.2.cloned.1.call-update) | async-done | bytes 2097168 | tf_op jit(solution)/shard_map/all_gather | solution.py:118
  63.7 97.2 %while.15 = (s32[]{:T(128)}, bf16[4,8,64,512]{3,2,1,0:T(8,128)(2,1)}, f32[4,8,64,8]{2,3,1,0:T(8,128)}, f32[4,8,64,8]{2,3,1,0:T(8,128)}, s32[4,8]{1,0:T(4,128)S(1...) while((s32[]{:T(128)}, ...), condition=%wide.region_3.4_spmd.clone, body=%wide.region_0.3_spmd.clone.sunk | while | flops 565184128 | bytes 43791872 | solution.py:125
  162.6 5.1 all-to-all-start.1
  171.4 3.6 all-to-all-done.1
  175.0 4.0 all-to-all-start
  182.3 4.1 all-to-all-done
  186.4 4.7 all-to-all-start.2
  209.7 5.9 %mul.135 = f32[32,64,8,64]{3,2,1,0:T(8,128)} broadcast(f32[32,64,8]{2,1,0:T(8,128)} %copy.92), dimensions={0,1,2} | broadcast | bytes 4259840 | tf_op jit(solution)/shard_map/mul | solution.py:166
  215.7 7.5 %mul.136 = f32[32,1,64,512]{3,2,1,0:T(8,128)} reshape(f32[32,64,8,64]{3,2,1,0:T(8,128)} %mul.135) | data formatting | bytes 8388608 | tf_op jit(solution)/shard_map/mul | solution.py:166
  223.2 3.6 multiply_reduce_fusion
  238.3 60.7 %all-reduce.3.cloned.1.call-done = f32[64,2880]{1,0:T(8,128)} async-done(((f32[64,2880]{1,0:T(8,128)}), f32[64,2880]{1,0:T(8,128)}) %all-reduce.3.cloned.1.call-update) | async-done | bytes 737296 | tf_op jit(solution)/shard_map/psum | solution.py:179
  304.0 4.6 copy.103
  308.5 50.3 %all_to_all.25 = bf16[32,16,2880]{2,1,0:T(8,128)(2,1)S(1)} all-to-all(bf16[32,16,2880]{2,1,0:T(8,128)(2,1)} %bitcast.319), channel_id=1, replica_groups=mesh['seq'=32,'tp'=8] {'seq'}, dimensions={0} | all-to-all | bytes 5898240 | tf_op jit(solution)/shard_map/all_to_all | solution.py:210
  360.4 4.2 fusion.27
  364.7 8.5 %convolution_convert_fusion = bf16[32,16,2880]{2,1,0:T(8,128)(2,1)} fusion(bf16[1,360,2880]{2,1,0:T(8,128)(2,1)} %param.32, bf16[32,16,2880]{2,1,0:T(8,128)(2,1)} %copy-done.2, bf16[1,2,2880,360]{2,3,1,0:T(8,128)(2,1)} %param.31, f32[32,1,16,360]{3,2,0,1:T(8,128)} %fusion.27), kind=kOutput, calls=%fused_computation.41 | convolution fusion | flops 2126315520 | bytes 10989568 | tf_op jit(solution)/shard_map/sexf,efd->sexd/dot_general | solution.py:88
  373.2 21.4 %copy.108 = bf16[32,16,2880]{1,0,2:T(8,128)(2,1)} copy(bf16[32,16,2880]{2,1,0:T(8,128)(2,1)} %convolution_convert_fusion) | data formatting | bytes 5898240
  394.5 39.5 %reshape.807 = bf16[2880,512]{1,0:T(8,128)(2,1)} reshape(bf16[2880,32,16]{2,1,0:T(8,128)(2,1)} %bitcast.316) | data formatting | bytes 5898240
  435.7 22.6 %all_gather.7 = bf16[32,16,1,128]{3,1,2,0:T(8,128)(2,1)S(1)} all-gather(bf16[1,16,1,128]{3,1,2,0:T(8,128)(2,1)S(1)} %bitcast_select_fusion.2), channel_id=1, replica_groups=mesh['seq'=32,'tp'=8] {'seq'}, dimensions={0}, use_global_device_ids=true | all-gather | bytes 135168 | tf_op jit(solution)/shard_map/all_gather | solution.py:227
  458.5 12.3 %reduce-scatter.4.cloned.1.call-done = bf16[360,512]{1,0:T(8,128)(2,1)} async-done(((bf16[2880,512]{1,0:T(8,128)(2,1)}), bf16[360,512]{1,0:T(8,128)(2,1)}) %reduce-scatter.4.cloned.1.call-update) | async-done | bytes 368656
  470.8 4.4 reshape.808
  475.1 5.0 copy.109
  480.2 11.2 %all-to-all-start.4 = ((bf16[32,16,360]{2,1,0:T(8,128)(2,1)}), bf16[32,16,360]{2,1,0:T(8,128)(2,1)S(1)}, u32[]{:S(2)}, u32[]{:S(2)}) async-start(bf16[32,16,360]{2,1,0:T(8,128)(2,1)} %copy.109), calls=%async_computation.4 | async-start | bytes 786432 | tf_op jit(solution)/shard_map/all_to_all | solution.py:217
  492.8 8.7 %all-to-all-done.4 = bf16[32,16,360]{2,1,0:T(8,128)(2,1)S(1)} async-done(((bf16[32,16,360]{2,1,0:T(8,128)(2,1)}), bf16[32,16,360]{2,1,0:T(8,128)(2,1)S(1)}, u32[]{:S(2)}, u32[]{:S(2)}) %all-to-all-start.4) | async-done | bytes 368672 | tf_op jit(solution)/shard_map/all_to_all | solution.py:217
  (219 shorter events, 161.5 us)
Async XLA Ops:
  7.2 219.6 %copy-start = (bf16[512,2880]{0,1:T(8,128)(2,1)S(1)}, bf16[512,2880]{0,1:T(8,128)(2,1)}, u32[]{:S(2)}) copy-start(bf16[512,2880]{0,1:T(8,128)(2,1)} %param.26) | copy-start | bytes 8847364
  7.2 56.5 %all-gather.2.cloned.1.call-start = ((), (), s32[]{:S(2)}) async-start(), calls=%async_computation.6 | async-start | bytes 2162688 | tf_op jit(solution)/shard_map/all_gather | solution.py:118
  7.9 16.3 %collective-permute-start = (bf16[64,360]{1,0:T(8,128)(2,1)}, bf16[64,360]{1,0:T(8,128)(2,1)}, u32[]{:S(2)}, u32[]{:S(2)}) collective-permute-start(bf16[64,360]{1,0:T(8,128)(2,1)} %param.27), channel_id=1, source_target_pairs={{0,1},{1,2},{2,3},{3,4},{4,5},{5,6},{6,7},{7,0},{8,9},{9,10},{10,1... | collective-permute-start | bytes 138248 | tf_op jit(solution)/shard_map/ppermute | solution.py:24
  10.5 168.7 %collective-permute-start.4 = (bf16[64,360]{1,0:T(8,128)(2,1)}, bf16[64,360]{1,0:T(8,128)(2,1)}, u32[]{:S(2)}, u32[]{:S(2)}) collective-permute-start(bf16[64,360]{1,0:T(8,128)(2,1)} %param.27), channel_id=1, source_target_pairs={{1,0},{2,1},{3,2},{4,3},{5,4},{6,5},{7,6},{0,7},{9,8},{10,9},{11,1... | collective-permute-start | bytes 138248 | tf_op jit(solution)/shard_map/ppermute | solution.py:26
  24.2 144.3 %collective-permute-start.1 = (bf16[64,360]{1,0:T(8,128)(2,1)}, bf16[64,360]{1,0:T(8,128)(2,1)}, u32[]{:S(2)}, u32[]{:S(2)}) collective-permute-start(bf16[64,360]{1,0:T(8,128)(2,1)} %collective-permute-done), channel_id=1, source_target_pairs={{0,1},{1,2},{2,3},{3,4},{4,5},{5,6},{6,7},{7,0},{8,9},{9,10},{10,1... | collective-permute-start | bytes 138248 | tf_op jit(solution)/shard_map/ppermute | solution.py:24
  160.9 30.3 %copy-start.4 = (f32[1,64,1,8,64]{4,1,3,2,0:T(8,128)S(1)}, f32[1,64,1,8,64]{4,1,3,2,0:T(8,128)}, u32[]{:S(2)}) copy-start(f32[1,64,1,8,64]{4,1,3,2,0:T(8,128)} %convolution_bitcast_fusion) | copy-start | bytes 393220
  162.6 12.4 %all-to-all-start.1 = ((f32[32,1,512]{2,1,0:T(1,128)}), f32[32,1,512]{2,1,0:T(1,128)S(1)}, u32[]{:S(2)}, u32[]{:S(2)}) async-start(f32[32,1,512]{2,1,0:T(1,128)} %reshape.812), calls=%async_computation.1 | async-start | bytes 131072 | tf_op jit(solution)/shard_map/all_to_all | solution.py:133
  168.5 13.8 %collective-permute-start.2 = (bf16[64,360]{1,0:T(8,128)(2,1)}, bf16[64,360]{1,0:T(8,128)(2,1)}, u32[]{:S(2)}, u32[]{:S(2)}) collective-permute-start(bf16[64,360]{1,0:T(8,128)(2,1)} %collective-permute-done.1), channel_id=1, source_target_pairs={{0,1},{1,2},{2,3},{3,4},{4,5},{5,6},{6,7},{7,0},{8,9},{9,10},{10,1... | collective-permute-start | bytes 138248 | tf_op jit(solution)/shard_map/ppermute | solution.py:24
  175.0 11.4 %all-to-all-start = ((f32[32,1,512]{2,1,0:T(1,128)}), f32[32,1,512]{2,1,0:T(1,128)S(1)}, u32[]{:S(2)}, u32[]{:S(2)}) async-start(f32[32,1,512]{2,1,0:T(1,128)} %reshape.810), calls=%async_computation | async-start | bytes 131072 | tf_op jit(solution)/shard_map/all_to_all | solution.py:134
  179.1 13.1 %collective-permute-start.5 = (bf16[64,360]{1,0:T(8,128)(2,1)}, bf16[64,360]{1,0:T(8,128)(2,1)}, u32[]{:S(2)}, u32[]{:S(2)}) collective-permute-start(bf16[64,360]{1,0:T(8,128)(2,1)} %collective-permute-done.4), channel_id=1, source_target_pairs={{1,0},{2,1},{3,2},{4,3},{5,4},{6,5},{7,6},{0,7},{9,8},{10,9},{11,1... | collective-permute-start | bytes 138248 | tf_op jit(solution)/shard_map/ppermute | solution.py:26
  182.3 12.9 %collective-permute-start.3 = (bf16[64,360]{1,0:T(8,128)(2,1)}, bf16[64,360]{1,0:T(8,128)(2,1)}, u32[]{:S(2)}, u32[]{:S(2)}) collective-permute-start(bf16[64,360]{1,0:T(8,128)(2,1)} %collective-permute-done.2), channel_id=1, source_target_pairs={{0,1},{1,2},{2,3},{3,4},{4,5},{5,6},{6,7},{7,0},{8,9},{9,10},{10,1... | collective-permute-start | bytes 138248 | tf_op jit(solution)/shard_map/ppermute | solution.py:24
  186.4 4.8 copy-start.9
  186.4 36.7 %all-to-all-start.2 = ((bf16[32,1,64,512]{3,2,1,0:T(8,128)(2,1)}), bf16[32,1,64,512]{3,2,1,0:T(8,128)(2,1)}, u32[]{:S(2)}, u32[]{:S(2)}) async-start(bf16[32,1,64,512]{3,2,1,0:T(8,128)(2,1)} %bitcast.323), calls=%async_computation.2 | async-start | bytes 4194304 | tf_op jit(solution)/shard_map/all_to_all | solution.py:131
  191.2 107.8 %all-reduce.3.cloned.1.call-start = ((), (), s32[]{:S(2)}) async-start(), calls=%async_computation.7 | async-start | bytes 1507328 | tf_op jit(solution)/shard_map/psum | solution.py:179
  192.2 39.4 %collective-permute-start.6 = (bf16[64,360]{1,0:T(8,128)(2,1)}, bf16[64,360]{1,0:T(8,128)(2,1)}, u32[]{:S(2)}, u32[]{:S(2)}) collective-permute-start(bf16[64,360]{1,0:T(8,128)(2,1)} %collective-permute-done.5), channel_id=1, source_target_pairs={{1,0},{2,1},{3,2},{4,3},{5,4},{6,5},{7,6},{0,7},{9,8},{10,9},{11,1... | collective-permute-start | bytes 138248 | tf_op jit(solution)/shard_map/ppermute | solution.py:26
  223.1 3.6 copy-start.7
  228.7 242.1 %reduce-scatter.4.cloned.1.call-start = ((), (), s32[]{:S(2)}) async-start(), calls=%async_computation.8 | async-start | bytes 3317760
  234.6 66.7 %copy-start.5 = (s32[512,64]{0,1:T(8,128)S(1)}, s32[512,64]{0,1:T(8,128)}, u32[]{:S(2)}) copy-start(s32[512,64]{0,1:T(8,128)} %convert_reduce_fusion) | copy-start | bytes 393220
  234.6 66.7 %copy-start.11 = (f32[2880]{0:T(1024)S(1)}, f32[2880]{0:T(1024)}, u32[]{:S(2)}) copy-start(f32[2880]{0:T(1024)} %param.28) | copy-start | bytes 34564
  394.5 39.5 %copy-start.10 = (s32[64,4]{0,1:T(4,128)S(1)}, s32[64,4]{0,1:T(4,128)}, u32[]{:S(2)}) copy-start(s32[64,4]{0,1:T(4,128)} %param.29) | copy-start | bytes 3076
  434.0 24.3 %copy-start.14 = (s32[32]{0:T(128)S(1)}, s32[32]{0:T(128)}, u32[]{:S(2)}) copy-start(s32[32]{0:T(128)} %param.35) | copy-start | bytes 388
  458.5 33.0 %copy-start.13 = (pred[64,4]{0,1:T(4,128)(4,1)S(1)}, pred[64,4]{0,1:T(4,128)(4,1)}, u32[]{:S(2)}) copy-start(pred[64,4]{0,1:T(4,128)(4,1)} %get-tuple-element.131) | copy-start | bytes 772
  458.5 33.1 %copy-start.12 = (f32[64,4]{0,1:T(4,128)S(1)}, f32[64,4]{0,1:T(4,128)}, u32[]{:S(2)}) copy-start(f32[64,4]{0,1:T(4,128)} %param.30) | copy-start | bytes 3076
  480.2 21.4 %all-to-all-start.4 = ((bf16[32,16,360]{2,1,0:T(8,128)(2,1)}), bf16[32,16,360]{2,1,0:T(8,128)(2,1)S(1)}, u32[]{:S(2)}, u32[]{:S(2)}) async-start(bf16[32,16,360]{2,1,0:T(8,128)(2,1)} %copy.109), calls=%async_computation.4 | async-start | bytes 786432 | tf_op jit(solution)/shard_map/all_to_all | solution.py:217
  (9 other events, 19.6 us)
Sparse Core Ops, SparseCore 0:
  10.6 53.0 all-gather.1
  228.8 70.1 all-reduce.2
  434.2 36.5 reduce-scatter.3
